TPU v7x, 32 devices: a whole 2x2x4 slice. The times are simulated.
32 devices in a mesh: dp: 4 (over x, core), row: 4 (over z), col: 2 (over y).
Axes of the slice: x: 2, y: 2, z: 4, core: 2. Of those that a mesh axis runs over, the one named last changes fastest.
Arguments:
- tokens_in: bfloat16 [8192, 768], P(('dp', 'col'), 'row'), may hold values from -6 to 6
- out_cot: bfloat16 [8192, 768], P(('dp', 'col'), 'row'), may hold values from -6 to 6
- segments: int32 [16, 512], P('dp'), may hold values from 0 to 31, never falling along the last dimension, each value on 1 to 256 neighbouring positions
- norm_params: float32 [4, 768], P(None, 'row'), may hold values from -1.2 to 1.5, as said below
- qkv_weight: float32 [768, 2304], P('row', 'col'), may hold values from -0.21875 to 0.21875
- proj_weight: float32 [768, 768], P('col', 'row'), may hold values from -0.875 to 0.875
- up_weight: float32 [768, 3072], P('row', 'col'), may hold values from -0.21875 to 0.21875
- down_weight: float32 [3072, 768], P('col', 'row'), may hold values from -0.109375 to 0.109375
- norm_first: float32 [4, 768], P(None, 'row'), may hold values from -18 to 18
- norm_second: float32 [4, 768], P(None, 'row'), may hold values from 30 to 300
- qkv_first: float32 [768, 2304], P('row', 'col'), may hold values from -18 to 18
- qkv_second: float32 [768, 2304], P('row', 'col'), may hold values from 30 to 300
- proj_first: float32 [768, 768], P('col', 'row'), may hold values from -18 to 18
- proj_second: float32 [768, 768], P('col', 'row'), may hold values from 30 to 300
- up_first: float32 [768, 3072], P('row', 'col'), may hold values from -18 to 18
- up_second: float32 [768, 3072], P('row', 'col'), may hold values from 30 to 300
- down_first: float32 [3072, 768], P('col', 'row'), may hold values from -18 to 18
- down_second: float32 [3072, 768], P('col', 'row'), may hold values from 30 to 300
Outputs:
- output: bfloat16 [8192, 768], P(('dp', 'col'), 'row')
- input_grad: bfloat16 [8192, 768], P(('dp', 'col'), 'row')
- norm_grad: float32 [4, 768], P(None, 'row')
- qkv_grad: float32 [768, 2304], P('row', 'col')
- proj_grad: float32 [768, 768], P('col', 'row')
- up_grad: float32 [768, 3072], P('row', 'col')
- down_grad: float32 [3072, 768], P('col', 'row')
- norm_new: float32 [4, 768], P(None, 'row')
- qkv_new: float32 [768, 2304], P('row', 'col')
- proj_new: float32 [768, 768], P('col', 'row')
- up_new: float32 [768, 3072], P('row', 'col')
- down_new: float32 [3072, 768], P('col', 'row')
- norm_first_new: float32 [4, 768], P(None, 'row')
- norm_second_new: float32 [4, 768], P(None, 'row')
- qkv_first_new: float32 [768, 2304], P('row', 'col')
- qkv_second_new: float32 [768, 2304], P('row', 'col')
- proj_first_new: float32 [768, 768], P('col', 'row')
- proj_second_new: float32 [768, 768], P('col', 'row')
- up_first_new: float32 [768, 3072], P('row', 'col')
- up_second_new: float32 [768, 3072], P('row', 'col')
- down_first_new: float32 [3072, 768], P('col', 'row')
- down_second_new: float32 [3072, 768], P('col', 'row')
Inputs may be any that keep to these rules, and one draw needn't show every extreme that they name: `segments`: within a row the numbers never fall; no number covers more than 256 positions of a row, and one covers exactly that many. `norm_params`: rows 0 and 2 lie in 0.5 to 1.5.
All inputs are finite; a program needn't handle non-finite values.
Results may differ from a plain program's by a relative error of at most 0.0093.
Values may be sent and summed in bfloat16 or wider, within the bound.
A program may use at most 192 MiB of HBM per device.

v0:
```python
import math
import jax
import jax.numpy as jnp
from jax import lax
from jax.sharding import PartitionSpec as P

D = 768
HEAD_DIM = 64
ROT_DIM = 16
SEQ_LEN = 512
STEP = 3
norm_eps = 1e-05
rotary_base = 10000.0
learn_rate = 0.01
beta_first = 0.9
beta_second = 0.95
adam_eps = 1e-08
decay_rate = 0.1
mask_fill = -1e30
inv_sqrt_two = 0.7071067811865476
inv_sqrt_two_pi = 0.3989422804014327


def gelu_value(value):
    return 0.5 * value * (1.0 + lax.erf(value * inv_sqrt_two))


def gelu_slope(value):
    return 0.5 * (1.0 + lax.erf(value * inv_sqrt_two)) + value * inv_sqrt_two_pi * jnp.exp(
        -0.5 * value * value
    )


def positions_of(segs):
    length = segs.shape[-1]
    index = jnp.broadcast_to(jnp.arange(length, dtype=jnp.int32), segs.shape)
    starts = jnp.concatenate(
        [jnp.ones(segs.shape[:-1] + (1,), bool), segs[..., 1:] != segs[..., :-1]], -1
    )
    first = lax.cummax(jnp.where(starts, index, 0), axis=segs.ndim - 1)
    return index - first


def rotary_tables(positions):
    half = ROT_DIM // 2
    freq = rotary_base ** (-2.0 * jnp.arange(half, dtype=jnp.float32) / ROT_DIM)
    angle = positions.astype(jnp.float32)[..., None] * freq
    return (jnp.cos(angle), jnp.sin(angle))


def rotate(tensor, cosine, sine):
    half = ROT_DIM // 2
    cos_part = cosine[..., None, :]
    sin_part = sine[..., None, :]
    front = tensor[..., :half]
    back = tensor[..., half:ROT_DIM]
    return jnp.concatenate(
        [
            front * cos_part - back * sin_part,
            back * cos_part + front * sin_part,
            tensor[..., ROT_DIM:],
        ],
        -1,
    )


def rotate_back(grad, cosine, sine):
    half = ROT_DIM // 2
    cos_part = cosine[..., None, :]
    sin_part = sine[..., None, :]
    front = grad[..., :half]
    back = grad[..., half:ROT_DIM]
    return jnp.concatenate(
        [
            front * cos_part + back * sin_part,
            back * cos_part - front * sin_part,
            grad[..., ROT_DIM:],
        ],
        -1,
    )


def masked_scores(query, keys, segment):
    length = segment.shape[0]
    scores = jnp.einsum(
        "qhd,khd->hqk", query, keys, preferred_element_type=jnp.float32
    ) / math.sqrt(HEAD_DIM)
    index = jnp.arange(length, dtype=jnp.int32)
    allowed = (segment[:, None] == segment[None, :]) & (index[None, :] <= index[:, None])
    return jnp.where(allowed[None], scores, mask_fill)


def attend(query, keys, values, segment):
    scores = masked_scores(query, keys, segment)
    total = jnp.sum(jnp.exp(scores), -1, keepdims=True)
    logsum = jnp.log(total)
    weights = jnp.exp(scores - logsum).astype(jnp.bfloat16)
    mixed = jnp.einsum("hqk,khd->qhd", weights, values, preferred_element_type=jnp.float32).astype(
        jnp.bfloat16
    )
    return (mixed, logsum[..., 0])


def attend_back(query, keys, values, segment, logsum, mixed, grad_mixed):
    scores = masked_scores(query, keys, segment)
    probs = jnp.exp(scores - logsum[..., None])
    weights = probs.astype(jnp.bfloat16)
    value_grad = jnp.einsum("hqk,qhd->khd", weights, grad_mixed, preferred_element_type=jnp.float32)
    prod_grad = jnp.einsum("qhd,khd->hqk", grad_mixed, values, preferred_element_type=jnp.float32)
    delta = jnp.sum(grad_mixed.astype(jnp.float32) * mixed.astype(jnp.float32), -1).T
    score_grad = (probs * (prod_grad - delta[..., None]) / math.sqrt(HEAD_DIM)).astype(jnp.bfloat16)
    query_grad = jnp.einsum("hqk,khd->qhd", score_grad, keys, preferred_element_type=jnp.float32)
    key_grad = jnp.einsum("hqk,qhd->khd", score_grad, query, preferred_element_type=jnp.float32)
    return (query_grad, key_grad, value_grad)


def dot32(left, right):
    return jnp.dot(left, right, preferred_element_type=jnp.float32)


def dot_rows(left, right):
    return lax.dot_general(
        left, right, (((0,), (0,)), ((), ())), preferred_element_type=jnp.float32
    )


def dot_cols(left, right):
    return lax.dot_general(
        left, right, (((1,), (1,)), ((), ())), preferred_element_type=jnp.float32
    )


def adam_update(weight, first, second, grad, decay):
    first_new = beta_first * first + (1.0 - beta_first) * grad
    second_new = beta_second * second + (1.0 - beta_second) * grad * grad
    first_hat = first_new / (1.0 - beta_first**STEP)
    second_hat = second_new / (1.0 - beta_second**STEP)
    weight_new = weight - learn_rate * (
        first_hat / (jnp.sqrt(second_hat) + adam_eps) + decay * weight
    )
    return (weight_new, first_new, second_new)


def gather_weight(piece):
    rows = piece.shape[0] // lax.axis_size("dp")
    own = lax.dynamic_slice_in_dim(piece, lax.axis_index("dp") * rows, rows, 0)
    return lax.all_gather(own, ("row", "dp"), axis=0, tiled=True)


def reduce_weights(grads):
    whole = jnp.concatenate([grad.astype(jnp.bfloat16) for grad in grads], 1)
    part = lax.psum_scatter(whole, ("row", "dp"), scatter_dimension=0, tiled=True)
    sums, start = ([], 0)
    for grad in grads:
        piece = part[:, start : start + grad.shape[1]]
        sums.append(lax.all_gather(piece, "dp", axis=0, tiled=True).astype(jnp.float32))
        start += grad.shape[1]
    return sums


def on_device(
    tokens_in,
    out_cot,
    segments,
    norm_params,
    qkv_weight,
    proj_weight,
    up_weight,
    down_weight,
    norm_first,
    norm_second,
    qkv_first,
    qkv_second,
    proj_first,
    proj_second,
    up_first,
    up_second,
    down_first,
    down_second,
):
    row_count = lax.axis_size("row")
    row_index = lax.axis_index("row")
    col_count = lax.axis_size("col")
    col_index = lax.axis_index("col")
    local_count, local_width = tokens_in.shape
    heads_here = qkv_weight.shape[1] // (3 * HEAD_DIM)
    seq_count = segments.shape[0] // row_count
    group_count = local_count * col_count
    share = group_count // row_count
    width = local_width * row_count
    bf16 = jnp.bfloat16

    def to_tokens(rows):
        blocks = rows.reshape(row_count, share, local_width)
        blocks = lax.all_to_all(blocks, "row", 0, 0, tiled=True)
        return jnp.moveaxis(blocks, 0, 1).reshape(share, width)

    x16 = to_tokens(lax.all_gather(tokens_in, "col", axis=0, tiled=True))
    cot16 = to_tokens(lax.all_gather(out_cot, "col", axis=0, tiled=True))
    norm_full = lax.all_gather(norm_params, "row", axis=1, tiled=True)
    pieces = (qkv_weight, up_weight, proj_weight.T, down_weight.T)
    all16 = gather_weight(jnp.concatenate([piece.astype(bf16) for piece in pieces], 1))
    first_cut = qkv_weight.shape[1]
    second_cut = first_cut + up_weight.shape[1]
    qkv16 = all16[:, :first_cut]
    up16 = all16[:, first_cut:second_cut]
    out16 = all16[:, second_cut:]
    xfull = x16.astype(jnp.float32)
    mean = jnp.sum(xfull, 1, keepdims=True) / D
    spread = jnp.sum(xfull * xfull, 1, keepdims=True) / D - mean * mean
    rstd = lax.rsqrt(spread + norm_eps)
    normed = (xfull - mean) * rstd
    first_in = (normed * norm_full[0] + norm_full[1]).astype(bf16)
    second_in = (normed * norm_full[2] + norm_full[3]).astype(bf16)
    qkv_own = dot32(first_in, qkv16)
    hidden_here = dot32(second_in, up16)
    width_qkv = qkv16.shape[1]
    seg_own = lax.dynamic_slice_in_dim(segments, row_index * seq_count, seq_count, 0)
    cosine, sine = rotary_tables(positions_of(seg_own))
    packed = qkv_own.reshape(seq_count, SEQ_LEN, heads_here, 3, HEAD_DIM)
    query = rotate(packed[..., 0, :], cosine, sine).astype(bf16)
    keys = rotate(packed[..., 1, :], cosine, sine).astype(bf16)
    values = packed[..., 2, :].astype(bf16)
    attended, logsum = lax.map(lambda item: attend(*item), (query, keys, values, seg_own))
    attn_width = heads_here * HEAD_DIM
    attn_flat = attended.reshape(share, attn_width)
    active = gelu_value(hidden_here).astype(bf16)
    act_cat = jnp.concatenate([attn_flat, active], 1)
    out_part = dot_cols(act_cat, out16)
    out_grad = dot_rows(cot16, act_cat)
    act_grad = dot32(cot16, out16)
    attended_grad = act_grad[:, :attn_width].astype(bf16)
    hidden_grad = (act_grad[:, attn_width:] * gelu_slope(hidden_here)).astype(bf16)
    up_grad = dot_rows(second_in, hidden_grad)
    grad_heads = attended_grad.reshape(seq_count, SEQ_LEN, heads_here, HEAD_DIM)
    query_grad, key_grad, value_grad = lax.map(
        lambda item: attend_back(*item),
        (query, keys, values, seg_own, logsum, attended, grad_heads),
    )
    query_grad = rotate_back(query_grad, cosine, sine)
    key_grad = rotate_back(key_grad, cosine, sine)
    packed_grad = (
        jnp.stack([query_grad, key_grad, value_grad], 3).reshape(share, width_qkv).astype(bf16)
    )
    qkv_grad = dot_rows(first_in, packed_grad)
    qkv_grad, up_grad, out_grad = reduce_weights((qkv_grad, up_grad, out_grad))
    first_grad = dot_cols(packed_grad, qkv16)
    second_grad = dot_cols(hidden_grad, up16)
    norm_part = jnp.stack(
        [
            jnp.sum(first_grad * normed, 0),
            jnp.sum(first_grad, 0),
            jnp.sum(second_grad * normed, 0),
            jnp.sum(second_grad, 0),
        ],
        0,
    )
    combined = norm_full[0] * first_grad + norm_full[2] * second_grad
    back_first = jnp.sum(combined, 1, keepdims=True) / D
    back_second = jnp.sum(combined * normed, 1, keepdims=True) / D
    grad_part = rstd * (combined - back_first - normed * back_second)

    def to_features(part):
        blocks = part.astype(bf16).reshape(share, row_count, local_width)
        blocks = lax.all_to_all(jnp.moveaxis(blocks, 1, 0), "row", 0, 0, tiled=True)
        parts = blocks.reshape(col_count, local_count, local_width)
        total = lax.dynamic_index_in_dim(parts, col_index, 0, keepdims=False).astype(jnp.float32)
        for step in range(1, col_count):
            peer = lax.rem(col_index + step, col_count)
            sent = lax.dynamic_index_in_dim(parts, peer, 0, keepdims=False)
            ring = [(i, (i + step) % col_count) for i in range(col_count)]
            total = total + lax.ppermute(sent, "col", ring).astype(jnp.float32)
        return total

    output = (tokens_in.astype(jnp.float32) + to_features(out_part)).astype(bf16)
    input_grad = (out_cot.astype(jnp.float32) + to_features(grad_part)).astype(bf16)
    norm_grad = lax.dynamic_slice_in_dim(
        lax.psum(norm_part, ("dp", "row", "col")), row_index * local_width, local_width, 1
    )
    proj_grad = out_grad[:, :attn_width].T
    down_grad = out_grad[:, attn_width:].T
    norm_new, norm_first_new, norm_second_new = adam_update(
        norm_params, norm_first, norm_second, norm_grad, 0.0
    )
    qkv_new, qkv_first_new, qkv_second_new = adam_update(
        qkv_weight, qkv_first, qkv_second, qkv_grad, decay_rate
    )
    proj_new, proj_first_new, proj_second_new = adam_update(
        proj_weight, proj_first, proj_second, proj_grad, decay_rate
    )
    up_new, up_first_new, up_second_new = adam_update(
        up_weight, up_first, up_second, up_grad, decay_rate
    )
    down_new, down_first_new, down_second_new = adam_update(
        down_weight, down_first, down_second, down_grad, decay_rate
    )
    return (
        output,
        input_grad,
        norm_grad,
        qkv_grad,
        proj_grad,
        up_grad,
        down_grad,
        norm_new,
        qkv_new,
        proj_new,
        up_new,
        down_new,
        norm_first_new,
        norm_second_new,
        qkv_first_new,
        qkv_second_new,
        proj_first_new,
        proj_second_new,
        up_first_new,
        up_second_new,
        down_first_new,
        down_second_new,
    )


def solution(mesh):
    placed = (
        P(("dp", "col"), "row"),
        P(("dp", "col"), "row"),
        P("dp", None),
        P(None, "row"),
        P("row", "col"),
        P("col", "row"),
        P("row", "col"),
        P("col", "row"),
        P(None, "row"),
        P(None, "row"),
        P("row", "col"),
        P("row", "col"),
        P("col", "row"),
        P("col", "row"),
        P("row", "col"),
        P("row", "col"),
        P("col", "row"),
        P("col", "row"),
    )
    return jax.shard_map(
        on_device,
        mesh=mesh,
        in_specs=placed,
        out_specs=(
            P(("dp", "col"), "row"),
            P(("dp", "col"), "row"),
            P(None, "row"),
            P("row", "col"),
            P("col", "row"),
            P("row", "col"),
            P("col", "row"),
            P(None, "row"),
            P("row", "col"),
            P("col", "row"),
            P("row", "col"),
            P("col", "row"),
            P(None, "row"),
            P(None, "row"),
            P("row", "col"),
            P("row", "col"),
            P("col", "row"),
            P("col", "row"),
            P("row", "col"),
            P("row", "col"),
            P("col", "row"),
            P("col", "row"),
        ),
        check_vma=False,
    )
```

profile of v0, /device:TPU:0, one launch (start us, length us, event | category | flops | bytes accessed | tf_op | source)
XLA Modules:
  0.0 313.0 jit_solution(11491301340539677173)
XLA Ops:
  10.9 12.8 %all_gather.21 = bf16[2048,192]{0,1:T(8,128)(2,1)S(1)} all-gather(bf16[1024,192]{0,1:T(8,128)(2,1)S(1)} %copy-done.13), channel_id=1, replica_groups=mesh['dp'=4,'row'=4,'col'=2] {'col'}, dimensions={0}, use_global_device_ids=true | all-gather | bytes 1179648 | tf_op jit(solution)/shard_map/all_gather | solution.py:198
  24.7 5.1 %all-to-all-start = ((bf16[4,512,192]{1,2,0:T(8,128)(2,1)}), bf16[4,512,192]{1,2,0:T(8,128)(2,1)S(1)}, u32[]{:S(2)}, u32[]{:S(2)}) async-start(bf16[4,512,192]{1,2,0:T(8,128)(2,1)} %bitcast.147), calls=%async_computation | async-start | bytes 1572864 | tf_op jit(solution)/shard_map/all_to_all | solution.py:195
  29.8 40.2 %all-gather = f32[4,192,4]{1,2,0:T(4,128)S(1)} all-gather(f32[1,192,4]{1,2,0:T(4,128)S(1)} %bitcast.167), channel_id=1, replica_groups=mesh['dp'=4,'row'=4,'col'=2] {'row'}, dimensions={0}, use_global_device_ids=true | all-gather | bytes 15360 | tf_op jit(solution)/shard_map/all_gather | solution.py:200
  71.1 8.4 %all_gather.24 = bf16[2048,192]{0,1:T(8,128)(2,1)S(1)} all-gather(bf16[1024,192]{0,1:T(8,128)(2,1)S(1)} %copy-done.11), channel_id=1, replica_groups=mesh['dp'=4,'row'=4,'col'=2] {'col'}, dimensions={0}, use_global_device_ids=true | all-gather | bytes 1179648 | tf_op jit(solution)/shard_map/all_gather | solution.py:199
  82.8 4.2 %all-to-all-start.2 = ((bf16[4,512,192]{1,2,0:T(8,128)(2,1)}), bf16[4,512,192]{1,2,0:T(8,128)(2,1)}, u32[]{:S(2)}, u32[]{:S(2)}) async-start(bf16[4,512,192]{1,2,0:T(8,128)(2,1)} %bitcast.146), calls=%async_computation.2 | async-start | bytes 1572864 | tf_op jit(solution)/shard_map/all_to_all | solution.py:195
  99.0 4.2 %all-to-all-done.2 = bf16[4,512,192]{1,2,0:T(8,128)(2,1)} async-done(((bf16[4,512,192]{1,2,0:T(8,128)(2,1)}), bf16[4,512,192]{1,2,0:T(8,128)(2,1)}, u32[]{:S(2)}, u32[]{:S(2)}) %all-to-all-start.2) | async-done | bytes 786464 | tf_op jit(solution)/shard_map/all_to_all | solution.py:195
  103.2 3.9 %convolution_bitcast_fusion = f32[512,1920]{1,0:T(8,128)S(1)} fusion(bf16[512,768]{0,1:T(8,128)(2,1)} %bitcast.31, bf16[768,4608]{1,0:T(8,128)(2,1)} %all-gather.3.cloned.1.call-done), kind=kOutput, calls=%fused_computation.12 | convolution fusion | flops 1509949440 | bytes 7667712 | tf_op jit(solution)/shard_map/dot_general | solution.py:118
  109.8 7.4 %fusion.1 = f32[6,512,512]{1,2,0:T(8,128)} fusion(pred[512,512]{0,1:T(8,128)(4,1)} %fusion.38, bf16[512,6,48]{0,2,1:T(8,128)(2,1)S(1)} %get-tuple-element.202, bf16[512,6,8]{0,2,1:T(8,128)(2,1)S(1)} %get-tuple-element.193, bf16[512,6,8]{0,2,1:T(8,128)(2,1)S(1)} %get-tuple-element.194, bf16[512,6,48]{0,2,1:T(8,128)(2,1)S(1)} %get-tuple-element.201, ...), kind=kOutput, calls=%fused_computation.3 | convolution fusion | flops 415239680 | bytes 7340032 | tf_op jit(solution)/shard_map/while/body/eval_jaxpr/reduce_sum | solution.py:95
  117.2 4.3 %multiply_reduce_fusion.4 = (f32[512,6]{0,1:T(8,128)S(1)}, bf16[6,64,512]{2,1,0:T(8,128)(2,1)}) fusion(bf16[512,6,64]{0,2,1:T(8,128)(2,1)S(1)} %bitcast.152, f32[6,512,512]{1,2,0:T(8,128)} %fusion.1, f32[1,512,6,3,64]{1,4,3,2,0:T(8,128)S(1)} %copy-done.8), kind=kOutput, calls=%fused_computation.92 | convolution fusion | flops 203879424 | bytes 7483392 | tf_op jit(solution)/shard_map/while/body/eval_jaxpr/hqk,khd->qhd/dot_general | solution.py:98
  132.3 5.9 %fusion.9 = (bf16[512,1536]{1,0:T(8,128)(2,1)S(1)}, bf16[512,1536]{1,0:T(8,128)(2,1)}) fusion(f32[512,1920]{1,0:T(8,128)} %copy-done.30, bf16[768,4608]{1,0:T(8,128)(2,1)} %all-gather.3.cloned.1.call-done, f32[512,768]{1,0:T(8,128)S(1)} %copy-done.2, f32[768]{0:T(1024)S(1)} %copy-done.41, f32[768]{0:T(1024)S(1)} %copy-done.40, f32[512]{0:T(512)S(1)} %copy-done.34, ...), kind=kOutput, calls=%fused_computation.17 | convolution fusion | flops 1220149248 | bytes 10233856 | tf_op jit(solution)/shard_map/dot_general | solution.py:118
  145.4 3.5 %fusion.13 = bf16[768,1920]{0,1:T(8,128)(2,1)S(1)} fusion(bf16[512,768]{0,1:T(8,128)(2,1)} %bitcast.31, bf16[512,1536]{1,0:T(8,128)(2,1)} %get-tuple-element.176, bf16[512,384]{1,0:T(8,128)(2,1)S(1)} %copy.202), kind=kOutput, calls=%fused_computation.23 | convolution fusion | flops 1515356160 | bytes 5701632 | tf_op jit(solution)/shard_map/dot_general | solution.py:122
  148.9 3.4 %pad_maximum_fusion = bf16[768,4608]{0,1:T(8,128)(2,1)} fusion(bf16[768,1920]{0,1:T(8,128)(2,1)S(1)} %fusion.13, bf16[768,1536]{0,1:T(8,128)(2,1)S(1)} %copy.216, bf16[768,1152]{0,1:T(8,128)(2,1)S(1)} %copy-done.1), kind=kLoop, calls=%fused_computation.1 | loop fusion | flops 21233664 | bytes 14155776 | tf_op jit(solution)/shard_map/concatenate | solution.py:151
  152.3 10.3 %copy.228 = bf16[768,4608]{1,0:T(8,128)(2,1)} copy(bf16[768,4608]{0,1:T(8,128)(2,1)} %pad_maximum_fusion) | data formatting | bytes 14155776
  164.0 3.2 %fusion.17 = f32[512,768]{1,0:T(8,128)S(1)} fusion(bf16[512,1536]{1,0:T(8,128)(2,1)S(1)} %copy-done.45, bf16[768,4608]{1,0:T(8,128)(2,1)} %all-gather.3.cloned.1.call-done), kind=kOutput, calls=%fused_computation.28 | convolution fusion | flops 1207959552 | bytes 5505024 | tf_op jit(solution)/shard_map/dot_general | solution.py:128
  167.3 3.5 %multiply_reduce_fusion.1 = (f32[768]{0:T(1024)S(1)}, f32[512]{0:T(512)S(1)}, f32[768]{0:T(1024)S(1)}, f32[768]{0:T(1024)S(1)}, f32[512]{0:T(512)S(1)}, /*index=5*/f32[768]{0:T(1024)S(1)}, f32[512,768]{1,0:T(8,128)S(1)}) fusion(f32[512,768]{1,0:T(8,128)S(1)} %copy-done.3, f32[512]{0:T(512)S(1)} %copy-done.34, f32[512]{0:T(512)S(1)} %copy-done.32, ...), kind=kOutput, calls=%fused_computation.42 | convolution fusion | flops 911470592 | bytes 7694336 | tf_op jit(solution)/shard_map/dot_general | solution.py:128
  172.4 3.5 %all-to-all-start.3 = ((bf16[4,512,192]{1,2,0:T(8,128)(2,1)}), bf16[4,512,192]{1,2,0:T(8,128)(2,1)S(1)}, u32[]{:S(2)}, u32[]{:S(2)}) async-start(bf16[4,512,192]{1,2,0:T(8,128)(2,1)} %bitcast.47), calls=%async_computation.3 | async-start | bytes 1572864 | tf_op jit(solution)/shard_map/all_to_all | solution.py:265
  175.9 4.5 %fusion.27 = bf16[512,768]{1,0:T(8,128)(2,1)S(1)} fusion(bf16[768,4608]{1,0:T(8,128)(2,1)} %all-gather.3.cloned.1.call-done, bf16[512,1536]{1,0:T(8,128)(2,1)} %get-tuple-element.176, bf16[512,384]{1,0:T(8,128)(2,1)S(1)} %copy.202), kind=kOutput, calls=%fused_computation.57 | convolution fusion | flops 1514274816 | bytes 5701632 | tf_op jit(solution)/shard_map/dot_general | solution.py:128
  181.6 11.4 %all-to-all-done.3 = bf16[4,512,192]{1,2,0:T(8,128)(2,1)S(1)} async-done(((bf16[4,512,192]{1,2,0:T(8,128)(2,1)}), bf16[4,512,192]{1,2,0:T(8,128)(2,1)S(1)}, u32[]{:S(2)}, u32[]{:S(2)}) %all-to-all-start.3) | async-done | bytes 786464 | tf_op jit(solution)/shard_map/all_to_all | solution.py:265
  193.0 3.7 %all-to-all-start.1 = ((bf16[4,512,192]{1,2,0:T(8,128)(2,1)}), bf16[4,512,192]{1,2,0:T(8,128)(2,1)S(1)}, u32[]{:S(2)}, u32[]{:S(2)}) async-start(bf16[4,512,192]{1,2,0:T(8,128)(2,1)} %bitcast.29), calls=%async_computation.1 | async-start | bytes 1572864 | tf_op jit(solution)/shard_map/all_to_all | solution.py:265
  201.5 57.3 %psum.7 = f32[4,768]{1,0:T(4,128)S(1)} all-reduce(f32[4,768]{1,0:T(4,128)S(1)} %pad_maximum_fusion.6), channel_id=1, replica_groups=mesh['dp'=4,'row'=4,'col'=2] {'dp','row','col'}, use_global_device_ids=true, to_apply=%region_12.13 | all-reduce | flops 3072 | bytes 24576 | tf_op jit(solution)/shard_map/psum | solution.py:278
  266.6 5.8 %collective-permute-done = bf16[1024,192]{0,1:T(8,128)(2,1)S(1)} collective-permute-done((bf16[1024,192]{0,1:T(8,128)(2,1)S(1)}, bf16[1024,192]{0,1:T(8,128)(2,1)S(1)}, u32[]{:S(2)}, u32[]{:S(2)}) %collective-permute-start) | collective-permute-done | bytes 393248 | tf_op jit(solution)/shard_map/ppermute | solution.py:272
  274.4 7.5 %all_gather.26 = bf16[192,1920]{1,0:T(8,128)(2,1)S(1)} all-gather(bf16[48,1920]{1,0:T(8,128)(2,1)S(1)} %slice.169), channel_id=1, replica_groups=mesh['dp'=4,'row'=4,'col'=2] {'dp'}, dimensions={0}, use_global_device_ids=true | all-gather | bytes 921600 | tf_op jit(solution)/shard_map/all_gather | solution.py:156
  282.0 7.8 %all_gather.27 = bf16[192,1536]{1,0:T(8,128)(2,1)S(1)} all-gather(bf16[48,1536]{1,0:T(8,128)(2,1)S(1)} %slice-done), channel_id=1, replica_groups=mesh['dp'=4,'row'=4,'col'=2] {'dp'}, dimensions={0}, use_global_device_ids=true | all-gather | bytes 737280 | tf_op jit(solution)/shard_map/all_gather | solution.py:156
  289.8 6.8 %all_gather.25 = bf16[192,1152]{1,0:T(8,128)(2,1)S(1)} all-gather(bf16[48,1152]{1,0:T(8,128)(2,1)S(1)} %slice-done.1), channel_id=1, replica_groups=mesh['dp'=4,'row'=4,'col'=2] {'dp'}, dimensions={0}, use_global_device_ids=true | all-gather | bytes 552960 | tf_op jit(solution)/shard_map/all_gather | solution.py:156
  (188 shorter events, 69.5 us)
Async XLA Ops:
  7.2 83.2 %all-gather.3.cloned.1.call-start = ((), (), s32[]{:S(2)}) async-start(), calls=%async_computation.5 | async-start | bytes 7520256 | tf_op jit(solution)/shard_map/all_gather | solution.py:147
  23.7 6.0 %copy-start.37 = (f32[4,192]{1,0:T(4,128)S(1)}, f32[4,192]{1,0:T(4,128)}, u32[]{:S(2)}) copy-start(f32[4,192]{1,0:T(4,128)} %param.21) | copy-start | bytes 9220
  23.7 46.3 %copy-start.39 = (s32[4,512]{1,0:T(4,128)S(1)}, s32[4,512]{1,0:T(4,128)}, u32[]{:S(2)}) copy-start(s32[4,512]{1,0:T(4,128)} %param.20) | copy-start | bytes 24580
  23.7 47.4 %copy-start.11 = (bf16[1024,192]{0,1:T(8,128)(2,1)S(1)}, bf16[1024,192]{0,1:T(8,128)(2,1)}, u32[]{:S(2)}) copy-start(bf16[1024,192]{0,1:T(8,128)(2,1)} %param.19) | copy-start | bytes 1179652
  24.7 58.1 %all-to-all-start = ((bf16[4,512,192]{1,2,0:T(8,128)(2,1)}), bf16[4,512,192]{1,2,0:T(8,128)(2,1)S(1)}, u32[]{:S(2)}, u32[]{:S(2)}) async-start(bf16[4,512,192]{1,2,0:T(8,128)(2,1)} %bitcast.147), calls=%async_computation | async-start | bytes 1572864 | tf_op jit(solution)/shard_map/all_to_all | solution.py:195
  71.1 23.7 %copy-start.35 = (f32[768]{0:T(1024)}, f32[768]{0:T(1024)S(1)}, u32[]{:S(2)}) copy-start(f32[768]{0:T(1024)S(1)} %get-tuple-element.150) | copy-start | bytes 9220
  82.8 20.4 %all-to-all-start.2 = ((bf16[4,512,192]{1,2,0:T(8,128)(2,1)}), bf16[4,512,192]{1,2,0:T(8,128)(2,1)}, u32[]{:S(2)}, u32[]{:S(2)}) async-start(bf16[4,512,192]{1,2,0:T(8,128)(2,1)} %bitcast.146), calls=%async_computation.2 | async-start | bytes 1572864 | tf_op jit(solution)/shard_map/all_to_all | solution.py:195
  87.0 186.4 %reduce-scatter.4.cloned.1.call-start = ((), (), s32[]{:S(2)}) async-start(), calls=%async_computation.6 | async-start | bytes 7520256
  89.2 5.6 %copy-start.31 = (f32[512]{0:T(512)}, f32[512]{0:T(512)S(1)}, u32[]{:S(2)}) copy-start(f32[512]{0:T(512)S(1)} %get-tuple-element.197) | copy-start | bytes 6148
  89.2 5.6 %copy-start.33 = (f32[512]{0:T(512)}, f32[512]{0:T(512)S(1)}, u32[]{:S(2)}) copy-start(f32[512]{0:T(512)S(1)} %get-tuple-element.198) | copy-start | bytes 6148
  109.7 7.4 %copy-start.8 = (f32[1,512,6,3,64]{1,4,3,2,0:T(8,128)S(1)}, f32[1,512,6,3,64]{1,4,3,2,0:T(8,128)}, u32[]{:S(2)}) copy-start(f32[1,512,6,3,64]{1,4,3,2,0:T(8,128)} %copy-done.7) | copy-start | bytes 7077892
  117.2 4.6 %copy-start = (f32[6,512,512]{1,2,0:T(8,128)S(1)}, f32[6,512,512]{1,2,0:T(8,128)}, u32[]{:S(2)}) copy-start(f32[6,512,512]{1,2,0:T(8,128)} %fusion.1) | copy-start | bytes 18874372
  172.4 20.6 %all-to-all-start.3 = ((bf16[4,512,192]{1,2,0:T(8,128)(2,1)}), bf16[4,512,192]{1,2,0:T(8,128)(2,1)S(1)}, u32[]{:S(2)}, u32[]{:S(2)}) async-start(bf16[4,512,192]{1,2,0:T(8,128)(2,1)} %bitcast.47), calls=%async_computation.3 | async-start | bytes 1572864 | tf_op jit(solution)/shard_map/all_to_all | solution.py:265
  193.0 65.7 %all-to-all-start.1 = ((bf16[4,512,192]{1,2,0:T(8,128)(2,1)}), bf16[4,512,192]{1,2,0:T(8,128)(2,1)S(1)}, u32[]{:S(2)}, u32[]{:S(2)}) async-start(bf16[4,512,192]{1,2,0:T(8,128)(2,1)} %bitcast.29), calls=%async_computation.1 | async-start | bytes 1572864 | tf_op jit(solution)/shard_map/all_to_all | solution.py:265
  199.5 65.1 %collective-permute-start.1 = (bf16[1024,192]{0,1:T(8,128)(2,1)S(1)}, bf16[1024,192]{0,1:T(8,128)(2,1)}, u32[]{:S(2)}, u32[]{:S(2)}) collective-permute-start(bf16[1024,192]{0,1:T(8,128)(2,1)S(1)} %bitcast.162), channel_id=1, source_target_pairs={{0,1},{1,0},{2,3},{3,2},{4,5},{5,4},{6,7},{7,6},{8,9},{9,8},{10,11... | collective-permute-start | bytes 1179656 | tf_op jit(solution)/shard_map/ppermute | solution.py:272
  259.9 4.0 %copy-start.38 = (f32[4,192]{1,0:T(4,128)S(1)}, f32[4,192]{1,0:T(4,128)}, u32[]{:S(2)}) copy-start(f32[4,192]{1,0:T(4,128)} %param.21) | copy-start | bytes 9220
  259.9 4.7 %copy-start.12 = (bf16[1024,192]{0,1:T(8,128)(2,1)S(1)}, bf16[1024,192]{0,1:T(8,128)(2,1)}, u32[]{:S(2)}) copy-start(bf16[1024,192]{0,1:T(8,128)(2,1)} %param.19) | copy-start | bytes 1179652
  261.4 11.1 %copy-start.14 = (bf16[1024,192]{0,1:T(8,128)(2,1)S(1)}, bf16[1024,192]{0,1:T(8,128)(2,1)}, u32[]{:S(2)}) copy-start(bf16[1024,192]{0,1:T(8,128)(2,1)} %param.18) | copy-start | bytes 1179652
  261.5 10.9 %collective-permute-start = (bf16[1024,192]{0,1:T(8,128)(2,1)S(1)}, bf16[1024,192]{0,1:T(8,128)(2,1)S(1)}, u32[]{:S(2)}, u32[]{:S(2)}) collective-permute-start(bf16[1024,192]{0,1:T(8,128)(2,1)S(1)} %bitcast.163), channel_id=1, source_target_pairs={{0,1},{1,0},{2,3},{3,2},{4,5},{5,4},{6,7},{7,6},{8,9},{9,8},{10,11... | collective-permute-start | bytes 1179656 | tf_op jit(solution)/shard_map/ppermute | solution.py:272
  274.4 7.6 %slice-start = ((bf16[48,4608]{1,0:T(8,128)(2,1)}), bf16[48,1536]{1,0:T(8,128)(2,1)S(1)}, s32[]{:S(2)}) async-start(bf16[48,4608]{1,0:T(8,128)(2,1)} %reduce-scatter.4.cloned.1.call-done), calls=%async_computation.7 | async-start | bytes 294912 | tf_op jit(solution)/shard_map/slice | solution.py:155
  274.4 15.4 %slice-start.1 = ((bf16[48,4608]{1,0:T(8,128)(2,1)}), bf16[48,1152]{1,0:T(8,128)(2,1)S(1)}, s32[]{:S(2)}) async-start(bf16[48,4608]{1,0:T(8,128)(2,1)} %reduce-scatter.4.cloned.1.call-done), calls=%async_computation.8 | async-start | bytes 221184 | tf_op jit(solution)/shard_map/slice | solution.py:155
  281.9 14.7 %copy-start.4 = (f32[1536,192]{0,1:T(8,128)S(1)}, f32[1536,192]{0,1:T(8,128)}, u32[]{:S(2)}) copy-start(f32[1536,192]{0,1:T(8,128)} %param.25) | copy-start | bytes 3538948
  281.9 14.7 %copy-start.15 = (f32[1536,192]{0,1:T(8,128)S(1)}, f32[1536,192]{0,1:T(8,128)}, u32[]{:S(2)}) copy-start(f32[1536,192]{0,1:T(8,128)} %param.34) | copy-start | bytes 3538948
  281.9 14.7 %copy-start.16 = (f32[1536,192]{0,1:T(8,128)S(1)}, f32[1536,192]{0,1:T(8,128)}, u32[]{:S(2)}) copy-start(f32[1536,192]{0,1:T(8,128)} %param.35) | copy-start | bytes 3538948
  (32 other events, 77.7 us)
Sparse Core Ops, SparseCore 0:
  10.9 76.4 all-gather.2
  162.7 102.5 reduce-scatter.3
where the time goes:
time: 317 us; the launch traced here: 313 us
  blocking collectives  141 us (44%)
  matrix products  47.2 us (15%)
  local copies, waits for them, and re-layouts  42.3 us (13%)
  other arithmetic  25.5 us (8%)
  waiting for transfers between devices  21.4 us (7%)
  starting transfers between devices  21 us (7%)
  between operations  15 us (5%)
    psum x1, blocking collectives, on_device(): lax.psum(norm_part, ('dp', 'row', 'col'))  57.3 us
    all_gather x1, blocking collectives, on_device(): norm_full = lax.all_gather(norm_params, 'row', axis=1, tiled=True)  40.2 us
    all_gather x3, blocking collectives, reduce_weights(): lax.all_gather(piece, 'dp', axis=0, tiled=True).astype(jnp.float32)  22.1 us
    unnamed x96, local copies, waits for them, and re-layouts  21 us
    all_gather x1, blocking collectives, on_device(): x16 = to_tokens(lax.all_gather(tokens_in, 'col', axis=0, tiled=True))  12.8 us
    dot_general x3, matrix products, dot32(): return jnp.dot(left, right, preferred_element_type=jnp.float32)  12.5 us
    all_to_all x2, waiting for transfers between devices, to_features(): blocks = lax.all_to_all(jnp.moveaxis(blocks, 1, 0), 'row', 0, 0, tiled=True)  11.4 us
    dot_general x3, matrix products, dot_cols(): lax.dot_general(left, right, (((1,), (1,)), ((), ())), preferred_element_...  11.3 us
  transfers between devices with their start and end apart: 8, of which 3 were waited for; matrix products, arithmetic and copies ran while one was open for 12% of the time, Pallas kernels for 0%

commit v1 on v0

--- a/solution.py
+++ b/solution.py
@@ -21,6 +21,17 @@
 inv_sqrt_two_pi = 0.3989422804014327
 
 
+def build_block(xin, ax_name):
+    chips = jax.lax.psum(1, ax_name)
+    chunks = [xin]
+    for p in range(1, chips):
+        chunks.append(
+            jax.lax.ppermute(chunks[p - 1], ax_name, [(b, (b - 1) % chips) for b in range(chips)])
+        )
+    current_value = jnp.concatenate(chunks, axis=0)
+    return jnp.roll(current_value, shift=jax.lax.axis_index(ax_name) * xin.shape[0], axis=0)
+
+
 def gelu_value(value):
     return 0.5 * value * (1.0 + lax.erf(value * inv_sqrt_two))
 
@@ -153,7 +164,7 @@
     sums, start = ([], 0)
     for grad in grads:
         piece = part[:, start : start + grad.shape[1]]
-        sums.append(lax.all_gather(piece, "dp", axis=0, tiled=True).astype(jnp.float32))
+        sums.append(build_block(piece, ax_name="dp").astype(jnp.float32))
         start += grad.shape[1]
     return sums
 

time: 317 us -> 313 us (0.987)
  blocking collectives: 141 us -> 119 us
  starting transfers between devices: 21 us -> 31.1 us
    all_gather x3 -> x0, blocking collectives: 22.1 us -> none  [reduce_weights(): lax.all_gather(piece, 'dp', axis=0, tiled=True).astype(jnp.float32)]
    ppermute x0 -> x9, starting transfers between devices: none -> 10.2 us  [build_block(): jax.lax.ppermute(chunks[p - 1], ax_name, [(b, (b - 1) % chips) for b in r...]
    unnamed x96 -> x116, local copies, waits for them, and re-layouts: 21 us -> 21.8 us
  transfers between devices with their start and end apart: 8 -> 17, of which waited for: 3 -> 7; matrix products, arithmetic and copies ran while one was open for 12% -> 15% of each run, Pallas kernels for 0% -> 0%
where the time goes in v1:
time: 313 us; the launch traced here: 308 us
  blocking collectives  119 us (38%)
  matrix products  47.5 us (15%)
  local copies, waits for them, and re-layouts  45.1 us (14%)
  starting transfers between devices  31.1 us (10%)
  other arithmetic  25.6 us (8%)
  waiting for transfers between devices  24.5 us (8%)
  between operations  15.2 us (5%)
    psum x1, blocking collectives, on_device(): lax.psum(norm_part, ('dp', 'row', 'col'))  57.2 us
    all_gather x1, blocking collectives, on_device(): norm_full = lax.all_gather(norm_params, 'row', axis=1, tiled=True)  40.2 us
    unnamed x116, local copies, waits for them, and re-layouts  21.8 us
    dot_general x3, matrix products, dot32(): return jnp.dot(left, right, preferred_element_type=jnp.float32)  12.8 us
    all_gather x1, blocking collectives, on_device(): x16 = to_tokens(lax.all_gather(tokens_in, 'col', axis=0, tiled=True))  12.8 us
    all_to_all x2, waiting for transfers between devices, to_features(): blocks = lax.all_to_all(jnp.moveaxis(blocks, 1, 0), 'row', 0, 0, tiled=True)  11.4 us
    dot_general x3, matrix products, dot_cols(): lax.dot_general(left, right, (((1,), (1,)), ((), ())), preferred_element_...  11.3 us
    ppermute x9, starting transfers between devices, build_block(): jax.lax.ppermute(chunks[p - 1], ax_name, [(b, (b - 1) % chips) for b in r...  10.2 us
  transfers between devices with their start and end apart: 17, of which 7 were waited for; matrix products, arithmetic and copies ran while one was open for 15% of the time, Pallas kernels for 0%

profile of v1, /device:TPU:0, one launch (start us, length us, event | category | flops | bytes accessed | tf_op | source)
XLA Modules:
  0.0 307.6 jit_solution(5688831458922785222)
XLA Ops:
  10.9 12.8 %all_gather.12 = bf16[2048,192]{0,1:T(8,128)(2,1)S(1)} all-gather(bf16[1024,192]{0,1:T(8,128)(2,1)S(1)} %copy-done.14), channel_id=1, replica_groups=mesh['dp'=4,'row'=4,'col'=2] {'col'}, dimensions={0}, use_global_device_ids=true | all-gather | bytes 1179648 | tf_op jit(solution)/shard_map/all_gather | solution.py:209
  24.7 5.1 %all-to-all-start = ((bf16[4,512,192]{1,2,0:T(8,128)(2,1)}), bf16[4,512,192]{1,2,0:T(8,128)(2,1)S(1)}, u32[]{:S(2)}, u32[]{:S(2)}) async-start(bf16[4,512,192]{1,2,0:T(8,128)(2,1)} %bitcast.147), calls=%async_computation | async-start | bytes 1572864 | tf_op jit(solution)/shard_map/all_to_all | solution.py:206
  29.8 40.2 %all-gather = f32[4,192,4]{1,2,0:T(4,128)S(1)} all-gather(f32[1,192,4]{1,2,0:T(4,128)S(1)} %bitcast.167), channel_id=1, replica_groups=mesh['dp'=4,'row'=4,'col'=2] {'row'}, dimensions={0}, use_global_device_ids=true | all-gather | bytes 15360 | tf_op jit(solution)/shard_map/all_gather | solution.py:211
  71.1 8.4 %all_gather.15 = bf16[2048,192]{0,1:T(8,128)(2,1)S(1)} all-gather(bf16[1024,192]{0,1:T(8,128)(2,1)S(1)} %copy-done.12), channel_id=1, replica_groups=mesh['dp'=4,'row'=4,'col'=2] {'col'}, dimensions={0}, use_global_device_ids=true | all-gather | bytes 1179648 | tf_op jit(solution)/shard_map/all_gather | solution.py:210
  82.8 4.2 %all-to-all-start.2 = ((bf16[4,512,192]{1,2,0:T(8,128)(2,1)}), bf16[4,512,192]{1,2,0:T(8,128)(2,1)}, u32[]{:S(2)}, u32[]{:S(2)}) async-start(bf16[4,512,192]{1,2,0:T(8,128)(2,1)} %bitcast.146), calls=%async_computation.2 | async-start | bytes 1572864 | tf_op jit(solution)/shard_map/all_to_all | solution.py:206
  94.7 2.7 convolution_bitcast_fusion.1
  98.9 4.3 %all-to-all-done.2 = bf16[4,512,192]{1,2,0:T(8,128)(2,1)} async-done(((bf16[4,512,192]{1,2,0:T(8,128)(2,1)}), bf16[4,512,192]{1,2,0:T(8,128)(2,1)}, u32[]{:S(2)}, u32[]{:S(2)}) %all-to-all-start.2) | async-done | bytes 786464 | tf_op jit(solution)/shard_map/all_to_all | solution.py:206
  103.2 3.9 %convolution_bitcast_fusion = f32[512,1920]{1,0:T(8,128)S(1)} fusion(bf16[512,768]{0,1:T(8,128)(2,1)} %bitcast.31, bf16[768,4608]{1,0:T(8,128)(2,1)} %all-gather.3.cloned.1.call-done), kind=kOutput, calls=%fused_computation.12 | convolution fusion | flops 1509949440 | bytes 7667712 | tf_op jit(solution)/shard_map/dot_general | solution.py:129
  109.7 7.4 %fusion.1 = f32[6,512,512]{1,2,0:T(8,128)} fusion(pred[512,512]{0,1:T(8,128)(4,1)} %fusion.38, bf16[512,6,48]{0,2,1:T(8,128)(2,1)S(1)} %get-tuple-element.230, bf16[512,6,8]{0,2,1:T(8,128)(2,1)S(1)} %get-tuple-element.221, bf16[512,6,8]{0,2,1:T(8,128)(2,1)S(1)} %get-tuple-element.222, bf16[512,6,48]{0,2,1:T(8,128)(2,1)S(1)} %get-tuple-element.229, ...), kind=kOutput, calls=%fused_computation.3 | convolution fusion | flops 415239680 | bytes 7340032 | tf_op jit(solution)/shard_map/while/body/eval_jaxpr/reduce_sum | solution.py:106
  117.2 4.3 %multiply_reduce_fusion.4 = (f32[512,6]{0,1:T(8,128)S(1)}, bf16[6,64,512]{2,1,0:T(8,128)(2,1)}) fusion(bf16[512,6,64]{0,2,1:T(8,128)(2,1)S(1)} %bitcast.152, f32[6,512,512]{1,2,0:T(8,128)} %fusion.1, f32[1,512,6,3,64]{1,4,3,2,0:T(8,128)S(1)} %copy-done.8), kind=kOutput, calls=%fused_computation.92 | convolution fusion | flops 203879424 | bytes 7483392 | tf_op jit(solution)/shard_map/while/body/eval_jaxpr/hqk,khd->qhd/dot_general | solution.py:109
  132.2 6.3 %fusion.9 = (bf16[512,1536]{1,0:T(8,128)(2,1)S(1)}, bf16[512,1536]{1,0:T(8,128)(2,1)}) fusion(f32[512,1920]{1,0:T(8,128)} %copy-done.31, bf16[768,4608]{1,0:T(8,128)(2,1)} %all-gather.3.cloned.1.call-done, f32[512,768]{1,0:T(8,128)S(1)} %copy-done.2, f32[768]{0:T(1024)S(1)} %copy-done.42, f32[768]{0:T(1024)S(1)} %copy-done.41, f32[512]{0:T(512)S(1)} %copy-done.35, ...), kind=kOutput, calls=%fused_computation.17 | convolution fusion | flops 1220149248 | bytes 10233856 | tf_op jit(solution)/shard_map/dot_general | solution.py:129
  139.7 3.2 %convolution_convert_fusion.1 = bf16[768,1536]{1,0:T(8,128)(2,1)} fusion(bf16[512,1536]{1,0:T(8,128)(2,1)S(1)} %get-tuple-element.197, f32[512,768]{1,0:T(8,128)S(1)} %copy-done.2, f32[768]{0:T(1024)S(1)} %copy-done.42, f32[768]{0:T(1024)S(1)} %copy-done.41, f32[512]{0:T(512)S(1)} %copy-done.35, f32[512]{0:T(512)S(1)} %copy-done.33), kind=kOutput, calls=%fused_computation.10 | convolution fusion | flops 1211105280 | bytes 5515264 | tf_op jit(solution)/shard_map/dot_general | solution.py:133
  142.9 2.8 copy.270
  145.7 3.5 %fusion.13 = bf16[768,1920]{0,1:T(8,128)(2,1)S(1)} fusion(bf16[512,768]{0,1:T(8,128)(2,1)} %bitcast.31, bf16[512,1536]{1,0:T(8,128)(2,1)} %get-tuple-element.198, bf16[512,384]{1,0:T(8,128)(2,1)S(1)} %copy.256), kind=kOutput, calls=%fused_computation.23 | convolution fusion | flops 1515356160 | bytes 5701632 | tf_op jit(solution)/shard_map/dot_general | solution.py:133
  149.2 3.4 %pad_maximum_fusion = bf16[768,4608]{0,1:T(8,128)(2,1)} fusion(bf16[768,1920]{0,1:T(8,128)(2,1)S(1)} %fusion.13, bf16[768,1536]{0,1:T(8,128)(2,1)S(1)} %copy.270, bf16[768,1152]{0,1:T(8,128)(2,1)S(1)} %copy-done.1), kind=kLoop, calls=%fused_computation.1 | loop fusion | flops 21233664 | bytes 14155776 | tf_op jit(solution)/shard_map/concatenate | solution.py:162
  152.7 10.2 %copy.282 = bf16[768,4608]{1,0:T(8,128)(2,1)} copy(bf16[768,4608]{0,1:T(8,128)(2,1)} %pad_maximum_fusion) | data formatting | bytes 14155776
  164.3 3.2 %fusion.17 = f32[512,768]{1,0:T(8,128)S(1)} fusion(bf16[512,1536]{1,0:T(8,128)(2,1)S(1)} %copy-done.46, bf16[768,4608]{1,0:T(8,128)(2,1)} %all-gather.3.cloned.1.call-done), kind=kOutput, calls=%fused_computation.28 | convolution fusion | flops 1207959552 | bytes 5505024 | tf_op jit(solution)/shard_map/dot_general | solution.py:139
  167.5 3.5 %multiply_reduce_fusion.1 = (f32[768]{0:T(1024)S(1)}, f32[512]{0:T(512)S(1)}, f32[768]{0:T(1024)S(1)}, f32[768]{0:T(1024)S(1)}, f32[512]{0:T(512)S(1)}, /*index=5*/f32[768]{0:T(1024)S(1)}, f32[512,768]{1,0:T(8,128)S(1)}) fusion(f32[512,768]{1,0:T(8,128)S(1)} %copy-done.3, f32[512]{0:T(512)S(1)} %copy-done.35, f32[512]{0:T(512)S(1)} %copy-done.33, ...), kind=kOutput, calls=%fused_computation.42 | convolution fusion | flops 911470592 | bytes 7694336 | tf_op jit(solution)/shard_map/dot_general | solution.py:139
  172.6 3.5 %all-to-all-start.3 = ((bf16[4,512,192]{1,2,0:T(8,128)(2,1)}), bf16[4,512,192]{1,2,0:T(8,128)(2,1)S(1)}, u32[]{:S(2)}, u32[]{:S(2)}) async-start(bf16[4,512,192]{1,2,0:T(8,128)(2,1)} %bitcast.47), calls=%async_computation.3 | async-start | bytes 1572864 | tf_op jit(solution)/shard_map/all_to_all | solution.py:276
  176.2 4.5 %fusion.27 = bf16[512,768]{1,0:T(8,128)(2,1)S(1)} fusion(bf16[768,4608]{1,0:T(8,128)(2,1)} %all-gather.3.cloned.1.call-done, bf16[512,1536]{1,0:T(8,128)(2,1)} %get-tuple-element.198, bf16[512,384]{1,0:T(8,128)(2,1)S(1)} %copy.256), kind=kOutput, calls=%fused_computation.57 | convolution fusion | flops 1514274816 | bytes 5701632 | tf_op jit(solution)/shard_map/dot_general | solution.py:139
  181.9 11.4 %all-to-all-done.3 = bf16[4,512,192]{1,2,0:T(8,128)(2,1)S(1)} async-done(((bf16[4,512,192]{1,2,0:T(8,128)(2,1)}), bf16[4,512,192]{1,2,0:T(8,128)(2,1)S(1)}, u32[]{:S(2)}, u32[]{:S(2)}) %all-to-all-start.3) | async-done | bytes 786464 | tf_op jit(solution)/shard_map/all_to_all | solution.py:276
  193.2 3.7 %all-to-all-start.1 = ((bf16[4,512,192]{1,2,0:T(8,128)(2,1)}), bf16[4,512,192]{1,2,0:T(8,128)(2,1)S(1)}, u32[]{:S(2)}, u32[]{:S(2)}) async-start(bf16[4,512,192]{1,2,0:T(8,128)(2,1)} %bitcast.29), calls=%async_computation.1 | async-start | bytes 1572864 | tf_op jit(solution)/shard_map/all_to_all | solution.py:276
  201.7 57.2 %psum.7 = f32[4,768]{1,0:T(4,128)S(1)} all-reduce(f32[4,768]{1,0:T(4,128)S(1)} %pad_maximum_fusion.6), channel_id=1, replica_groups=mesh['dp'=4,'row'=4,'col'=2] {'dp','row','col'}, use_global_device_ids=true, to_apply=%region_12.13 | all-reduce | flops 3072 | bytes 24576 | tf_op jit(solution)/shard_map/psum | solution.py:289
  266.8 5.8 %collective-permute-done = bf16[1024,192]{0,1:T(8,128)(2,1)S(1)} collective-permute-done((bf16[1024,192]{0,1:T(8,128)(2,1)S(1)}, bf16[1024,192]{0,1:T(8,128)(2,1)S(1)}, u32[]{:S(2)}, u32[]{:S(2)}) %collective-permute-start) | collective-permute-done | bytes 393248 | tf_op jit(solution)/shard_map/ppermute | solution.py:283
  (224 shorter events, 76.9 us)
Async XLA Ops:
  7.2 83.2 %all-gather.3.cloned.1.call-start = ((), (), s32[]{:S(2)}) async-start(), calls=%async_computation.5 | async-start | bytes 7520256 | tf_op jit(solution)/shard_map/all_gather | solution.py:158
  23.7 46.3 %copy-start.40 = (s32[4,512]{1,0:T(4,128)S(1)}, s32[4,512]{1,0:T(4,128)}, u32[]{:S(2)}) copy-start(s32[4,512]{1,0:T(4,128)} %param.20) | copy-start | bytes 24580
  23.7 47.4 %copy-start.12 = (bf16[1024,192]{0,1:T(8,128)(2,1)S(1)}, bf16[1024,192]{0,1:T(8,128)(2,1)}, u32[]{:S(2)}) copy-start(bf16[1024,192]{0,1:T(8,128)(2,1)} %param.19) | copy-start | bytes 1179652
  24.7 58.1 %all-to-all-start = ((bf16[4,512,192]{1,2,0:T(8,128)(2,1)}), bf16[4,512,192]{1,2,0:T(8,128)(2,1)S(1)}, u32[]{:S(2)}, u32[]{:S(2)}) async-start(bf16[4,512,192]{1,2,0:T(8,128)(2,1)} %bitcast.147), calls=%async_computation | async-start | bytes 1572864 | tf_op jit(solution)/shard_map/all_to_all | solution.py:206
  71.1 23.6 %copy-start.36 = (f32[768]{0:T(1024)}, f32[768]{0:T(1024)S(1)}, u32[]{:S(2)}) copy-start(f32[768]{0:T(1024)S(1)} %get-tuple-element.172) | copy-start | bytes 9220
  82.8 20.4 %all-to-all-start.2 = ((bf16[4,512,192]{1,2,0:T(8,128)(2,1)}), bf16[4,512,192]{1,2,0:T(8,128)(2,1)}, u32[]{:S(2)}, u32[]{:S(2)}) async-start(bf16[4,512,192]{1,2,0:T(8,128)(2,1)} %bitcast.146), calls=%async_computation.2 | async-start | bytes 1572864 | tf_op jit(solution)/shard_map/all_to_all | solution.py:206
  87.0 186.6 %reduce-scatter.4.cloned.1.call-start = ((), (), s32[]{:S(2)}) async-start(), calls=%async_computation.6 | async-start | bytes 7520256 | tf_op jit(solution)/shard_map/reduce_scatter | solution.py:163
  172.6 20.6 %all-to-all-start.3 = ((bf16[4,512,192]{1,2,0:T(8,128)(2,1)}), bf16[4,512,192]{1,2,0:T(8,128)(2,1)S(1)}, u32[]{:S(2)}, u32[]{:S(2)}) async-start(bf16[4,512,192]{1,2,0:T(8,128)(2,1)} %bitcast.47), calls=%async_computation.3 | async-start | bytes 1572864 | tf_op jit(solution)/shard_map/all_to_all | solution.py:276
  193.2 65.6 %all-to-all-start.1 = ((bf16[4,512,192]{1,2,0:T(8,128)(2,1)}), bf16[4,512,192]{1,2,0:T(8,128)(2,1)S(1)}, u32[]{:S(2)}, u32[]{:S(2)}) async-start(bf16[4,512,192]{1,2,0:T(8,128)(2,1)} %bitcast.29), calls=%async_computation.1 | async-start | bytes 1572864 | tf_op jit(solution)/shard_map/all_to_all | solution.py:276
  199.7 65.0 %collective-permute-start.1 = (bf16[1024,192]{0,1:T(8,128)(2,1)S(1)}, bf16[1024,192]{0,1:T(8,128)(2,1)}, u32[]{:S(2)}, u32[]{:S(2)}) collective-permute-start(bf16[1024,192]{0,1:T(8,128)(2,1)S(1)} %bitcast.162), channel_id=1, source_target_pairs={{0,1},{1,0},{2,3},{3,2},{4,5},{5,4},{6,7},{7,6},{8,9},{9,8},{10,11... | collective-permute-start | bytes 1179656 | tf_op jit(solution)/shard_map/ppermute | solution.py:283
  261.7 10.9 %collective-permute-start = (bf16[1024,192]{0,1:T(8,128)(2,1)S(1)}, bf16[1024,192]{0,1:T(8,128)(2,1)S(1)}, u32[]{:S(2)}, u32[]{:S(2)}) collective-permute-start(bf16[1024,192]{0,1:T(8,128)(2,1)S(1)} %bitcast.163), channel_id=1, source_target_pairs={{0,1},{1,0},{2,3},{3,2},{4,5},{5,4},{6,7},{7,6},{8,9},{9,8},{10,11... | collective-permute-start | bytes 1179656 | tf_op jit(solution)/shard_map/ppermute | solution.py:283
  273.6 13.9 %copy-start.11 = (bf16[48,4608]{1,0:T(8,128)(2,1)S(1)}, bf16[48,4608]{1,0:T(8,128)(2,1)}, u32[]{:S(2)}) copy-start(bf16[48,4608]{1,0:T(8,128)(2,1)} %reduce-scatter.4.cloned.1.call-done) | copy-start | bytes 1327108
  274.6 5.9 %collective-permute-start.8 = (bf16[48,1536]{1,0:T(8,128)(2,1)S(1)}, bf16[48,1536]{1,0:T(8,128)(2,1)S(1)}, u32[]{:S(2)}, u32[]{:S(2)}) collective-permute-start(bf16[48,1536]{1,0:T(8,128)(2,1)S(1)} %get-tuple-element.213), channel_id=1, source_target_pairs={{0,24},{8,0},{16,8},{24,16},{1,25},{9,1},{17,9},{25,17},{2,26},{10... | collective-permute-start | bytes 442376 | tf_op jit(solution)/shard_map/ppermute | solution.py:29
  275.6 12.0 %copy-start.10 = (f32[192,1152]{1,0:T(8,128)S(1)}, f32[192,1152]{1,0:T(8,128)}, u32[]{:S(2)}) copy-start(f32[192,1152]{1,0:T(8,128)} %param.22) | copy-start | bytes 2654212
  275.6 12.0 %copy-start.24 = (f32[192,1152]{1,0:T(8,128)S(1)}, f32[192,1152]{1,0:T(8,128)}, u32[]{:S(2)}) copy-start(f32[192,1152]{1,0:T(8,128)} %param.28) | copy-start | bytes 2654212
  275.6 12.0 %copy-start.25 = (f32[192,1152]{1,0:T(8,128)S(1)}, f32[192,1152]{1,0:T(8,128)}, u32[]{:S(2)}) copy-start(f32[192,1152]{1,0:T(8,128)} %param.29) | copy-start | bytes 2654212
  275.6 3.0 collective-permute-start.2
  277.4 3.3 %collective-permute-start.5 = (bf16[48,1920]{1,0:T(8,128)(2,1)S(1)}, bf16[48,1920]{1,0:T(8,128)(2,1)S(1)}, u32[]{:S(2)}, u32[]{:S(2)}) collective-permute-start(bf16[48,1920]{1,0:T(8,128)(2,1)S(1)} %get-tuple-element.215), channel_id=1, source_target_pairs={{0,24},{8,0},{16,8},{24,16},{1,25},{9,1},{17,9},{25,17},{2,26},{10... | collective-permute-start | bytes 552968 | tf_op jit(solution)/shard_map/ppermute | solution.py:29
  278.7 4.2 %collective-permute-start.3 = (bf16[48,1152]{1,0:T(8,128)(2,1)S(1)}, bf16[48,1152]{1,0:T(8,128)(2,1)S(1)}, u32[]{:S(2)}, u32[]{:S(2)}) collective-permute-start(bf16[48,1152]{1,0:T(8,128)(2,1)S(1)} %collective-permute-done.2), channel_id=1, source_target_pairs={{0,24},{8,0},{16,8},{24,16},{1,25},{9,1},{17,9},{25,17},{2,26},{10... | collective-permute-start | bytes 331784 | tf_op jit(solution)/shard_map/ppermute | solution.py:29
  280.6 4.2 %collective-permute-start.9 = (bf16[48,1536]{1,0:T(8,128)(2,1)S(1)}, bf16[48,1536]{1,0:T(8,128)(2,1)S(1)}, u32[]{:S(2)}, u32[]{:S(2)}) collective-permute-start(bf16[48,1536]{1,0:T(8,128)(2,1)S(1)} %collective-permute-done.8), channel_id=1, source_target_pairs={{0,24},{8,0},{16,8},{24,16},{1,25},{9,1},{17,9},{25,17},{2,26},{10... | collective-permute-start | bytes 442376 | tf_op jit(solution)/shard_map/ppermute | solution.py:29
  280.7 9.0 %collective-permute-start.6 = (bf16[48,1920]{1,0:T(8,128)(2,1)S(1)}, bf16[48,1920]{1,0:T(8,128)(2,1)S(1)}, u32[]{:S(2)}, u32[]{:S(2)}) collective-permute-start(bf16[48,1920]{1,0:T(8,128)(2,1)S(1)} %collective-permute-done.5), channel_id=1, source_target_pairs={{0,24},{8,0},{16,8},{24,16},{1,25},{9,1},{17,9},{25,17},{2,26},{10... | collective-permute-start | bytes 552968 | tf_op jit(solution)/shard_map/ppermute | solution.py:29
  282.9 4.7 %collective-permute-start.4 = (bf16[48,1152]{1,0:T(8,128)(2,1)S(1)}, bf16[48,1152]{1,0:T(8,128)(2,1)S(1)}, u32[]{:S(2)}, u32[]{:S(2)}) collective-permute-start(bf16[48,1152]{1,0:T(8,128)(2,1)S(1)} %collective-permute-done.3), channel_id=1, source_target_pairs={{0,24},{8,0},{16,8},{24,16},{1,25},{9,1},{17,9},{25,17},{2,26},{10... | collective-permute-start | bytes 331784 | tf_op jit(solution)/shard_map/ppermute | solution.py:29
  284.7 7.1 %collective-permute-start.10 = (bf16[48,1536]{1,0:T(8,128)(2,1)S(1)}, bf16[48,1536]{1,0:T(8,128)(2,1)S(1)}, u32[]{:S(2)}, u32[]{:S(2)}) collective-permute-start(bf16[48,1536]{1,0:T(8,128)(2,1)S(1)} %collective-permute-done.9), channel_id=1, source_target_pairs={{0,24},{8,0},{16,8},{24,16},{1,25},{9,1},{17,9},{25,17},{2,26},{10... | collective-permute-start | bytes 442376 | tf_op jit(solution)/shard_map/ppermute | solution.py:29
  289.7 5.2 %collective-permute-start.7 = (bf16[48,1920]{1,0:T(8,128)(2,1)S(1)}, bf16[48,1920]{1,0:T(8,128)(2,1)S(1)}, u32[]{:S(2)}, u32[]{:S(2)}) collective-permute-start(bf16[48,1920]{1,0:T(8,128)(2,1)S(1)} %collective-permute-done.6), channel_id=1, source_target_pairs={{0,24},{8,0},{16,8},{24,16},{1,25},{9,1},{17,9},{25,17},{2,26},{10... | collective-permute-start | bytes 552968 | tf_op jit(solution)/shard_map/ppermute | solution.py:29
  (40 other events, 126.7 us)
Sparse Core Ops, SparseCore 0:
  10.9 76.4 all-gather.2
  163.0 102.5 reduce-scatter.3
